TPU v7x, 512 devices: a whole 4x8x8 slice. The times are simulated.
512 devices in a mesh: interval: 8 (over y), seq: 8 (over x, core), head: 8 (over z).
Axes of the slice: x: 4, y: 8, z: 8, core: 2. Of those that a mesh axis runs over, the one named last changes fastest.
Arguments:
- hidden_in: bfloat16 [8, 2048, 1536], P('interval', 'seq'), may hold values from -6 to 6
- ctx_grad: bfloat16 [8, 2048, 1536], P('interval', 'seq', 'head'), may hold values from -6 to 6
- w_query: bfloat16 [1536, 1536], P('head'), may hold values from -0.15625 to 0.15625
- w_key: bfloat16 [1536, 1536], P('head'), may hold values from -0.15625 to 0.15625
- w_value: bfloat16 [1536, 1536], P('head'), may hold values from -0.15625 to 0.15625
- w_junction: bfloat16 [1536, 128], replicated, may hold values from -0.15625 to 0.15625
- donor_pos: int32 [8, 8, 8, 64], P('interval', 'seq', None, 'head'), may hold values from 0 to 255
- acceptor_pos: int32 [8, 8, 8, 64], P('interval', 'seq', None, 'head'), may hold values from 0 to 255
- junction_counts: int32 [8, 8, 8], P('interval', 'seq'), may hold values from 16 to 64, as said below
- pred_grad: float32 [8, 8, 8, 64], P('interval', 'seq', None, 'head'), may hold values from -6 to 6
Outputs:
- grad_input: bfloat16 [8, 2048, 1536], P('interval', 'seq', 'head')
- grad_query: bfloat16 [1536, 1536], P('head')
- grad_key: bfloat16 [1536, 1536], P('head')
- grad_value: bfloat16 [1536, 1536], P('head')
Inputs may be any that keep to these rules, and one draw needn't show every extreme that they name: `junction_counts`: slots at or past a bucket's count are empty. In each interval one acceptor shard, drawn from the seed, has 64 live slots from every donor shard; every other bucket has 16 to 32.
All inputs are finite; a program needn't handle non-finite values.
Results may differ from a plain program's by a relative error of at most 0.022.
Values may be sent and summed in bfloat16 or wider, within the bound.
No kernel may reach another device: no remote copies, remote signals or barrier semaphores. Data moves between devices by JAX's collectives and lax.ppermute only.
A program may use at most 64 MiB of HBM per device.

v0:
```python
import jax
import jax.numpy as jnp
from jax import lax
from jax.sharding import Mesh
from jax.sharding import PartitionSpec as P

HD = 192
PJ = 128
CORES = 2
F32 = jnp.float32
BF16 = jnp.bfloat16


def swap_cores(value):
    return lax.ppermute(value, "core", [(0, 1), (1, 0)])


def on_device(
    hidden_in,
    ctx_grad,
    w_query,
    w_key,
    w_value,
    w_junction,
    donor_pos,
    acceptor_pos,
    junction_counts,
    pred_grad,
):
    hidden = hidden_in[0]
    ctx = ctx_grad[0]
    tokens, width = hidden.shape
    chips = lax.axis_size("x")
    intervals = lax.axis_size("interval")
    core = lax.axis_index("core")
    half = chips * tokens
    softmax_scale = HD ** (-0.5)
    pair_scale = PJ ** (-0.5)

    def project(weight):
        return jnp.einsum("td,cd->tc", hidden, weight, preferred_element_type=F32).astype(BF16)

    queries, key_rows, value_rows = (project(w_query), project(w_key), project(w_value))
    features = jnp.dot(hidden, w_junction, preferred_element_type=F32).astype(BF16)
    sent = jnp.concatenate([key_rows, value_rows, features], axis=1)
    copies = jnp.broadcast_to(sent[None], (chips,) + sent.shape).reshape(half, -1)
    mine = lax.all_to_all(copies, "x", 0, 0, tiled=True)
    theirs = swap_cores(mine)
    both = jnp.concatenate([mine, theirs], axis=0)
    keys, values, all_features = (both[:, :HD], both[:, HD : 2 * HD], both[:, 2 * HD :])
    scores = jnp.einsum("qd,kd->qk", queries, keys, preferred_element_type=F32) * softmax_scale
    row_max = jnp.max(scores, axis=-1, keepdims=True)
    expd = jnp.exp(scores - row_max)
    probs = expd / jnp.sum(expd, axis=-1, keepdims=True)
    dprobs = jnp.einsum("qd,kd->qk", ctx, values, preferred_element_type=F32)
    row_delta = jnp.sum(probs * dprobs, axis=-1, keepdims=True)
    dscores_b = (probs * (dprobs - row_delta)).astype(BF16)
    probs_b = probs.astype(BF16)
    query_grad = (
        jnp.einsum("qk,kd->qd", dscores_b, keys, preferred_element_type=F32) * softmax_scale
    ).astype(BF16)
    key_term = (
        jnp.einsum("qk,qd->kd", dscores_b, queries, preferred_element_type=F32) * softmax_scale
    )
    value_term = jnp.einsum("qk,qd->kd", probs_b, ctx, preferred_element_type=F32)
    donor_idx = donor_pos[0, 0]
    buckets, slot_dev = donor_idx.shape
    slot_ids = lax.axis_index("head") * slot_dev + jnp.arange(slot_dev, dtype=jnp.int32)
    live_slots = slot_ids[None, :] < junction_counts[0, 0][:, None]
    shard = jnp.arange(buckets, dtype=jnp.int32)
    base = jnp.where(shard % CORES == core, 0, half) + shard // CORES * tokens
    accept_idx = base[:, None] + acceptor_pos[0, 0]
    donor_feat = features[donor_idx].astype(F32)
    accept_feat = all_features[accept_idx].astype(F32)
    pair_score = jnp.sum(donor_feat * accept_feat, axis=-1) * pair_scale
    slot_grad = (
        jnp.where(live_slots, pred_grad[0, 0] * jax.nn.sigmoid(pair_score), 0.0) * pair_scale
    )
    donor_term = slot_grad[..., None] * accept_feat
    accept_term = slot_grad[..., None] * donor_feat
    donor_sum = (
        jnp.zeros((tokens, PJ), F32).at[donor_idx.reshape(-1)].add(donor_term.reshape(-1, PJ))
    )
    spread = (
        jnp.zeros((CORES * half, PJ), F32)
        .at[accept_idx.reshape(-1)]
        .add(accept_term.reshape(-1, PJ))
    )
    terms = jnp.concatenate([key_term, value_term, spread], axis=1).astype(BF16)
    pair_sum = terms[:half].astype(F32) + swap_cores(terms[half:]).astype(F32)
    parts = lax.all_to_all(pair_sum.astype(BF16), "x", 0, 0, tiled=True)
    total = jnp.sum(parts.reshape(chips, tokens, -1).astype(F32), axis=0)
    key_grad = total[:, :HD].astype(BF16)
    value_grad = total[:, HD : 2 * HD].astype(BF16)
    feature_grad = (donor_sum + total[:, 2 * HD :]).astype(BF16)
    grads = jnp.concatenate([query_grad, key_grad, value_grad], axis=1)
    weights = jnp.concatenate([w_query, w_key, w_value], axis=0)
    input_term = jnp.dot(grads, weights, preferred_element_type=F32)
    input_term = input_term + jnp.einsum(
        "tp,dp->td", feature_grad, w_junction, preferred_element_type=F32
    )
    grad_input = lax.psum_scatter(input_term.astype(BF16), "head", scatter_dimension=1, tiled=True)
    rows = grads.shape[1]
    half_width = width // CORES
    weight_term = jnp.einsum("tc,td->cd", grads, hidden, preferred_element_type=F32).astype(BF16)

    def sum_parts(value, axis, count):
        got = lax.all_to_all(value, axis, 0, 0, tiled=True)
        return jnp.sum(got.reshape(count, -1, got.shape[-1]).astype(F32), axis=0).astype(BF16)

    term = weight_term.reshape(rows, CORES, half_width).transpose(1, 0, 2)
    term = sum_parts(term.reshape(CORES * rows, half_width), "core", CORES)
    term = sum_parts(term, "x", chips)
    part_rows = rows // chips
    cut = (2, part_rows // 2, intervals // 2, half_width // (intervals // 2))
    term = term.reshape(cut).transpose(0, 2, 1, 3).reshape(-1, cut[3])
    term = sum_parts(term, "interval", intervals)
    term = jnp.broadcast_to(term[None], (intervals,) + term.shape).reshape(-1, cut[3])
    term = lax.all_to_all(term, "interval", 0, 0, tiled=True)
    term = term.reshape(cut[0], cut[2], cut[1], cut[3]).transpose(0, 2, 1, 3)
    term = lax.all_gather(term.reshape(part_rows, half_width), "x", axis=0, tiled=True)
    other = swap_cores(term)
    left = jnp.where(core == 0, term, other)
    right = jnp.where(core == 0, other, term)
    whole = jnp.concatenate([left, right], axis=1)
    return (grad_input[None], whole[:HD], whole[HD : 2 * HD], whole[2 * HD :])


def solution(mesh):
    axes = (mesh.shape["interval"], mesh.shape["seq"] // CORES, CORES, mesh.shape["head"])
    split = Mesh(mesh.devices.reshape(axes), ("interval", "x", "core", "head"))
    seq = ("x", "core")
    placed = (
        P("interval", seq, None),
        P("interval", seq, "head"),
        P("head", None),
        P("head", None),
        P("head", None),
        P(),
        P("interval", seq, None, "head"),
        P("interval", seq, None, "head"),
        P("interval", seq, None),
        P("interval", seq, None, "head"),
    )
    return jax.shard_map(
        on_device,
        mesh=split,
        in_specs=placed,
        out_specs=(P("interval", seq, "head"), P("head", None), P("head", None), P("head", None)),
        check_vma=False,
    )
```

profile of v0, /device:TPU:2, one launch (start us, length us, event | category | flops | bytes accessed | tf_op | source)
XLA Modules:
  0.0 189.2 jit_solution(3122860435319958120)
XLA Ops:
  7.2 1.1 copy-done
  8.3 1.4 convolution_convert_fusion.5
  9.7 1.5 convolution_convert_fusion.2
  12.9 9.4 %all-to-all-start = ((bf16[4,256,512]{2,1,0:T(8,128)(2,1)}), bf16[4,256,512]{2,1,0:T(8,128)(2,1)S(1)}, u32[]{:S(2)}, u32[]{:S(2)}) async-start(bf16[4,256,512]{2,1,0:T(8,128)(2,1)} %broadcast_in_dim.17), calls=%async_computation | async-start | bytes 2097152 | tf_op jit(solution)/shard_map/all_to_all | solution.py:47
  22.3 9.4 %all-to-all-done = bf16[4,256,512]{2,1,0:T(8,128)(2,1)S(1)} async-done(((bf16[4,256,512]{2,1,0:T(8,128)(2,1)}), bf16[4,256,512]{2,1,0:T(8,128)(2,1)S(1)}, u32[]{:S(2)}, u32[]{:S(2)}) %all-to-all-start) | async-done | bytes 1048608 | tf_op jit(solution)/shard_map/all_to_all | solution.py:47
  31.7 1.9 %collective-permute-start = (bf16[1024,512]{1,0:T(8,128)(2,1)S(1)}, bf16[1024,512]{1,0:T(8,128)(2,1)S(1)}, u32[]{:S(2)}, u32[]{:S(2)}) collective-permute-start(bf16[1024,512]{1,0:T(8,128)(2,1)S(1)} %bitcast.71), channel_id=1, source_target_pairs={{0,8},{8,0},{1,9},{9,1},{2,10},{10,2},{3,11},{11,3},{4,12},{12,4},... | collective-permute-start | bytes 3145736 | tf_op jit(solution)/shard_map/ppermute | solution.py:15
  41.3 1.3 pad_clamp_fusion
  42.5 1.2 fusion.33
  45.6 1.5 convolution_convert_fusion.1
  49.7 1.3 fusion.1
  51.9 2.0 %scatter_custom_fusion = f32[2048,128]{1,0:T(8,128)} fusion(s32[64]{0:T(128)} %fusion.33, f32[]{:T(128)} %constant.30.clone.1, bf16[64,128]{1,0:T(8,128)(2,1)S(1)} %gather_fusion, f32[64]{0:T(128)S(1)} %fusion.35), kind=kCustom, calls=%fused_computation.56 | custom fusion | flops 24576 | bytes 1065728 | tf_op jit(solution)/shard_map/scatter-add | solution.py:87
  53.9 1.4 copy.45
  55.3 1.5 pad_maximum_fusion
  57.0 2.4 %collective-permute-start.1 = (bf16[1024,512]{0,1:T(8,128)(2,1)S(1)}, bf16[1024,512]{0,1:T(8,128)(2,1)S(1)}, u32[]{:S(2)}, u32[]{:S(2)}) collective-permute-start(bf16[1024,512]{0,1:T(8,128)(2,1)S(1)} %slice.56), channel_id=1, source_target_pairs={{0,8},{8,0},{1,9},{9,1},{2,10},{10,2},{3,11},{11,3},{4,12},{12,4},... | collective-permute-start | bytes 3145736 | tf_op jit(solution)/shard_map/ppermute | solution.py:15
  59.4 2.3 %collective-permute-done.1 = bf16[1024,512]{0,1:T(8,128)(2,1)S(1)} collective-permute-done((bf16[1024,512]{0,1:T(8,128)(2,1)S(1)}, bf16[1024,512]{0,1:T(8,128)(2,1)S(1)}, u32[]{:S(2)}, u32[]{:S(2)}) %collective-permute-start.1) | collective-permute-done | bytes 1048608 | tf_op jit(solution)/shard_map/ppermute | solution.py:15
  63.1 5.7 %all-to-all-start.1 = ((bf16[4,256,512]{1,2,0:T(8,128)(2,1)}), bf16[4,256,512]{1,2,0:T(8,128)(2,1)}, u32[]{:S(2)}, u32[]{:S(2)}) async-start(bf16[4,256,512]{1,2,0:T(8,128)(2,1)} %bitcast.79), calls=%async_computation.1 | async-start | bytes 2097152 | tf_op jit(solution)/shard_map/all_to_all | solution.py:91
  68.8 1.8 fusion.10
  70.6 12.8 %all-to-all-done.1 = bf16[4,256,512]{1,2,0:T(8,128)(2,1)} async-done(((bf16[4,256,512]{1,2,0:T(8,128)(2,1)}), bf16[4,256,512]{1,2,0:T(8,128)(2,1)}, u32[]{:S(2)}, u32[]{:S(2)}) %all-to-all-start.1) | async-done | bytes 1048608 | tf_op jit(solution)/shard_map/all_to_all | solution.py:91
  83.3 1.4 convert_reduce_fusion
  86.4 5.2 %all_to_all.48 = bf16[2,576,768]{2,1,0:T(8,128)(2,1)S(1)} all-to-all(bf16[2,576,768]{2,1,0:T(8,128)(2,1)S(1)} %bitcast.76), channel_id=1, replica_groups=mesh['interval'=8,'x'=4,'core'=2,'head'=8] {'core'}, dimensions={0} | all-to-all | bytes 3538944 | tf_op jit(solution)/shard_map/all_to_all | solution.py:108
  92.4 16.5 %all_to_all.49 = bf16[4,144,768]{2,1,0:T(8,128)(2,1)S(1)} all-to-all(bf16[4,144,768]{2,1,0:T(8,128)(2,1)S(1)} %bitcast.80), channel_id=1, replica_groups=mesh['interval'=8,'x'=4,'core'=2,'head'=8] {'x'}, dimensions={0} | all-to-all | bytes 1769472 | tf_op jit(solution)/shard_map/all_to_all | solution.py:108
  110.1 6.7 %all-to-all-start.4 = ((bf16[8,72,192]{2,1,0:T(8,128)(2,1)}), bf16[8,72,192]{2,1,0:T(8,128)(2,1)S(1)}, u32[]{:S(2)}, u32[]{:S(2)}) async-start(bf16[8,72,192]{2,1,0:T(8,128)(2,1)} %bitcast.13), calls=%async_computation.5 | async-start | bytes 589824 | tf_op jit(solution)/shard_map/all_to_all | solution.py:108
  118.1 10.8 %all-to-all-done.4 = bf16[8,72,192]{2,1,0:T(8,128)(2,1)S(1)} async-done(((bf16[8,72,192]{2,1,0:T(8,128)(2,1)}), bf16[8,72,192]{2,1,0:T(8,128)(2,1)S(1)}, u32[]{:S(2)}, u32[]{:S(2)}) %all-to-all-start.4) | async-done | bytes 221216 | tf_op jit(solution)/shard_map/all_to_all | solution.py:108
  129.7 3.4 %all-to-all-start.5 = ((bf16[8,72,192]{2,1,0:T(8,128)(2,1)}), bf16[8,72,192]{2,1,0:T(8,128)(2,1)S(1)}, u32[]{:S(2)}, u32[]{:S(2)}) async-start(bf16[8,72,192]{2,1,0:T(8,128)(2,1)} %broadcast_in_dim.23), calls=%async_computation.6 | async-start | bytes 589824 | tf_op jit(solution)/shard_map/all_to_all | solution.py:119
  133.2 2.0 %fusion.4 = f32[256,1536]{0,1:T(8,128)S(1)} fusion(bf16[192,1536]{1,0:T(8,128)(2,1)S(1)} %copy-done.6, bf16[192,1536]{1,0:T(8,128)(2,1)S(1)} %copy-done.8, bf16[192,1536]{1,0:T(8,128)(2,1)} %param.12, bf16[256,384]{0,1:T(8,128)(2,1)S(1)} %copy-done.5, bf16[256,192]{0,1:T(8,128)(2,1)S(1)} %fusion.10), kind=kOutput, calls=%fused_computation.29 | convolution fusion | flops 458883072 | bytes 3637248 | tf_op jit(solution)/shard_map/dot_general | solution.py:98
  135.3 1.2 fusion
  136.5 7.3 %all-to-all-done.5 = bf16[8,72,192]{2,1,0:T(8,128)(2,1)S(1)} async-done(((bf16[8,72,192]{2,1,0:T(8,128)(2,1)}), bf16[8,72,192]{2,1,0:T(8,128)(2,1)S(1)}, u32[]{:S(2)}, u32[]{:S(2)}) %all-to-all-start.5) | async-done | bytes 221216 | tf_op jit(solution)/shard_map/all_to_all | solution.py:119
  144.2 13.4 %all_gather.3 = bf16[576,768]{1,0:T(8,128)(2,1)S(1)} all-gather(bf16[144,768]{1,0:T(8,128)(2,1)S(1)} %reshape.268), channel_id=1, replica_groups=mesh['interval'=8,'x'=4,'core'=2,'head'=8] {'x'}, dimensions={0}, use_global_device_ids=true | all-gather | bytes 1105920 | tf_op jit(solution)/shard_map/all_gather | solution.py:121
  157.6 1.9 %collective-permute-start.2 = (bf16[576,768]{1,0:T(8,128)(2,1)S(1)}, bf16[576,768]{1,0:T(8,128)(2,1)S(1)}, u32[]{:S(2)}, u32[]{:S(2)}) collective-permute-start(bf16[576,768]{1,0:T(8,128)(2,1)S(1)} %all_gather.3), channel_id=1, source_target_pairs={{0,8},{8,0},{1,9},{9,1},{2,10},{10,2},{3,11},{11,3},{4,12},{12,4},... | collective-permute-start | bytes 2654216 | tf_op jit(solution)/shard_map/ppermute | solution.py:15
  159.6 2.4 %collective-permute-done.2 = bf16[576,768]{1,0:T(8,128)(2,1)S(1)} collective-permute-done((bf16[576,768]{1,0:T(8,128)(2,1)S(1)}, bf16[576,768]{1,0:T(8,128)(2,1)S(1)}, u32[]{:S(2)}, u32[]{:S(2)}) %collective-permute-start.2) | collective-permute-done | bytes 884768 | tf_op jit(solution)/shard_map/ppermute | solution.py:15
  162.1 1.2 pad_maximum_fusion.1
  163.3 19.0 %reduce-scatter.2.cloned.1.call-done = bf16[256,192]{0,1:T(8,128)(2,1)} async-done(((bf16[256,1536]{0,1:T(8,128)(2,1)}), bf16[256,192]{0,1:T(8,128)(2,1)}) %reduce-scatter.2.cloned.1.call-update) | async-done | bytes 98320 | tf_op jit(solution)/shard_map/reduce_scatter | solution.py:102
  (99 shorter events, 22.3 us)
Async XLA Ops:
  7.2 1.1 copy-start
  7.2 4.0 %copy-start.7 = (bf16[192,1536]{1,0:T(8,128)(2,1)S(1)}, bf16[192,1536]{1,0:T(8,128)(2,1)}, u32[]{:S(2)}) copy-start(bf16[192,1536]{1,0:T(8,128)(2,1)} %param.13) | copy-start | bytes 1769476
  9.7 1.9 %copy-start.10 = (bf16[256,128]{0,1:T(8,128)(2,1)}, bf16[256,128]{0,1:T(8,128)(2,1)S(1)}, u32[]{:S(2)}) copy-start(bf16[256,128]{0,1:T(8,128)(2,1)S(1)} %convolution_convert_fusion.5) | copy-start | bytes 196612
  11.7 22.0 %copy-start.12 = (s32[1,1,8,8]{3,2,1,0:T(8,128)S(1)}, s32[1,1,8,8]{3,2,1,0:T(8,128)}, u32[]{:S(2)}) copy-start(s32[1,1,8,8]{3,2,1,0:T(8,128)} %param.17) | copy-start | bytes 772
  11.7 24.2 %copy-start.13 = (s32[1,1,8,8]{3,2,1,0:T(8,128)S(1)}, s32[1,1,8,8]{3,2,1,0:T(8,128)}, u32[]{:S(2)}) copy-start(s32[1,1,8,8]{3,2,1,0:T(8,128)} %param.16) | copy-start | bytes 772
  11.7 26.3 %copy-start.17 = (f32[1,1,8,8]{3,2,1,0:T(8,128)S(1)}, f32[1,1,8,8]{3,2,1,0:T(8,128)}, u32[]{:S(2)}) copy-start(f32[1,1,8,8]{3,2,1,0:T(8,128)} %param.19) | copy-start | bytes 772
  11.7 32.0 %copy-start.9 = (bf16[192,1536]{1,0:T(8,128)(2,1)S(1)}, bf16[192,1536]{1,0:T(8,128)(2,1)}, u32[]{:S(2)}) copy-start(bf16[192,1536]{1,0:T(8,128)(2,1)} %param.12) | copy-start | bytes 1769476
  12.9 18.8 %all-to-all-start = ((bf16[4,256,512]{2,1,0:T(8,128)(2,1)}), bf16[4,256,512]{2,1,0:T(8,128)(2,1)S(1)}, u32[]{:S(2)}, u32[]{:S(2)}) async-start(bf16[4,256,512]{2,1,0:T(8,128)(2,1)} %broadcast_in_dim.17), calls=%async_computation | async-start | bytes 2097152 | tf_op jit(solution)/shard_map/all_to_all | solution.py:47
  22.3 11.4 %copy-start.21 = (s32[8]{0:T(128)}, s32[8]{0:T(128)S(1)}, u32[]{:S(2)}) copy-start(s32[8]{0:T(128)S(1)} %fusion.31) | copy-start | bytes 100
  31.7 12.4 %collective-permute-start = (bf16[1024,512]{1,0:T(8,128)(2,1)S(1)}, bf16[1024,512]{1,0:T(8,128)(2,1)S(1)}, u32[]{:S(2)}, u32[]{:S(2)}) collective-permute-start(bf16[1024,512]{1,0:T(8,128)(2,1)S(1)} %bitcast.71), channel_id=1, source_target_pairs={{0,8},{8,0},{1,9},{9,1},{2,10},{10,2},{3,11},{11,3},{4,12},{12,4},... | collective-permute-start | bytes 3145736 | tf_op jit(solution)/shard_map/ppermute | solution.py:15
  44.7 0.9 copy-start.22
  48.7 1.0 copy-start.1
  49.7 1.4 copy-start.11
  49.7 2.1 %copy-start.18 = (s32[64]{0:T(128)S(1)}, s32[64]{0:T(128)}, u32[]{:S(2)}) copy-start(s32[64]{0:T(128)} %lt.72) | copy-start | bytes 772
  49.7 2.1 %copy-start.19 = (s32[64]{0:T(128)S(1)}, s32[64]{0:T(128)}, u32[]{:S(2)}) copy-start(s32[64]{0:T(128)} %lt.75) | copy-start | bytes 772
  49.7 2.1 %copy-start.20 = (f32[64]{0:T(128)S(1)}, f32[64]{0:T(128)}, u32[]{:S(2)}) copy-start(f32[64]{0:T(128)} %squeeze.20) | copy-start | bytes 772
  51.9 5.0 %copy-start.15 = (f32[64]{0:T(128)}, f32[64]{0:T(128)S(1)}, u32[]{:S(2)}) copy-start(f32[64]{0:T(128)S(1)} %fusion.35) | copy-start | bytes 772
  57.0 4.7 %collective-permute-start.1 = (bf16[1024,512]{0,1:T(8,128)(2,1)S(1)}, bf16[1024,512]{0,1:T(8,128)(2,1)S(1)}, u32[]{:S(2)}, u32[]{:S(2)}) collective-permute-start(bf16[1024,512]{0,1:T(8,128)(2,1)S(1)} %slice.56), channel_id=1, source_target_pairs={{0,8},{8,0},{1,9},{9,1},{2,10},{10,2},{3,11},{11,3},{4,12},{12,4},... | collective-permute-start | bytes 3145736 | tf_op jit(solution)/shard_map/ppermute | solution.py:15
  63.1 20.2 %all-to-all-start.1 = ((bf16[4,256,512]{1,2,0:T(8,128)(2,1)}), bf16[4,256,512]{1,2,0:T(8,128)(2,1)}, u32[]{:S(2)}, u32[]{:S(2)}) async-start(bf16[4,256,512]{1,2,0:T(8,128)(2,1)} %bitcast.79), calls=%async_computation.1 | async-start | bytes 2097152 | tf_op jit(solution)/shard_map/all_to_all | solution.py:91
  84.8 0.8 copy-start.3
  85.6 0.7 copy-start.4
  92.4 24.4 %copy-start.14 = (s32[1,1,8,8]{3,2,1,0:T(8,128)S(1)}, s32[1,1,8,8]{3,2,1,0:T(8,128)}, u32[]{:S(2)}) copy-start(s32[1,1,8,8]{3,2,1,0:T(8,128)} %param.16) | copy-start | bytes 772
  92.4 24.5 %slice-start = ((f32[256,512]{0,1:T(8,128)}), f32[256,128]{0,1:T(8,128)S(1)}, s32[]{:S(2)}) async-start(f32[256,512]{0,1:T(8,128)} %copy-done.3), calls=%async_computation.8 | async-start | bytes 262144 | tf_op jit(solution)/shard_map/slice | solution.py:95
  108.9 8.1 %copy-start.16 = (f32[64]{0:T(128)S(1)}, f32[64]{0:T(128)}, u32[]{:S(2)}) copy-start(f32[64]{0:T(128)} %copy-done.15) | copy-start | bytes 772
  108.9 24.3 %copy-start.5 = (bf16[256,384]{0,1:T(8,128)(2,1)S(1)}, bf16[256,384]{0,1:T(8,128)(2,1)}, u32[]{:S(2)}) copy-start(bf16[256,384]{0,1:T(8,128)(2,1)} %copy-done.4) | copy-start | bytes 589828
  108.9 24.3 %copy-start.6 = (bf16[192,1536]{1,0:T(8,128)(2,1)S(1)}, bf16[192,1536]{1,0:T(8,128)(2,1)}, u32[]{:S(2)}) copy-start(bf16[192,1536]{1,0:T(8,128)(2,1)} %param.14) | copy-start | bytes 1769476
  109.1 24.1 %copy-start.8 = (bf16[192,1536]{1,0:T(8,128)(2,1)S(1)}, bf16[192,1536]{1,0:T(8,128)(2,1)}, u32[]{:S(2)}) copy-start(bf16[192,1536]{1,0:T(8,128)(2,1)} %param.13) | copy-start | bytes 1769476
  110.1 18.8 %all-to-all-start.4 = ((bf16[8,72,192]{2,1,0:T(8,128)(2,1)}), bf16[8,72,192]{2,1,0:T(8,128)(2,1)S(1)}, u32[]{:S(2)}, u32[]{:S(2)}) async-start(bf16[8,72,192]{2,1,0:T(8,128)(2,1)} %bitcast.13), calls=%async_computation.5 | async-start | bytes 589824 | tf_op jit(solution)/shard_map/all_to_all | solution.py:108
  129.7 14.2 %all-to-all-start.5 = ((bf16[8,72,192]{2,1,0:T(8,128)(2,1)}), bf16[8,72,192]{2,1,0:T(8,128)(2,1)S(1)}, u32[]{:S(2)}, u32[]{:S(2)}) async-start(bf16[8,72,192]{2,1,0:T(8,128)(2,1)} %broadcast_in_dim.23), calls=%async_computation.6 | async-start | bytes 589824 | tf_op jit(solution)/shard_map/all_to_all | solution.py:119
  133.1 2.1 %copy-start.2 = (bf16[1536,128]{1,0:T(8,128)(2,1)S(1)}, bf16[1536,128]{1,0:T(8,128)(2,1)}, u32[]{:S(2)}) copy-start(bf16[1536,128]{1,0:T(8,128)(2,1)} %param.15) | copy-start | bytes 1179652
  133.1 49.2 %reduce-scatter.2.cloned.1.call-start = ((), (), s32[]{:S(2)}) async-start(), calls=%async_computation.7 | async-start | bytes 884736 | tf_op jit(solution)/shard_map/reduce_scatter | solution.py:102
  157.6 4.3 %collective-permute-start.2 = (bf16[576,768]{1,0:T(8,128)(2,1)S(1)}, bf16[576,768]{1,0:T(8,128)(2,1)S(1)}, u32[]{:S(2)}, u32[]{:S(2)}) collective-permute-start(bf16[576,768]{1,0:T(8,128)(2,1)S(1)} %all_gather.3), channel_id=1, source_target_pairs={{0,8},{8,0},{1,9},{9,1},{2,10},{10,2},{3,11},{11,3},{4,12},{12,4},... | collective-permute-start | bytes 2654216 | tf_op jit(solution)/shard_map/ppermute | solution.py:15
Sparse Core Ops, SparseCore 0:
  137.4 44.9 reduce-scatter.1
where the time goes:
time: 190 us; the launch traced here: 189 us
  waiting for transfers between devices  64 us (34%)
  blocking collectives  35 us (18%)
  starting transfers between devices  31.5 us (17%)
  local copies, waits for them, and re-layouts  17.2 us (9%)
  between operations  14.5 us (8%)
  matrix products  13.7 us (7%)
  other arithmetic  13.2 us (7%)
    all_to_all x2, blocking collectives, sum_parts(): got = lax.all_to_all(value, axis, 0, 0, tiled=True)  21.6 us
    reduce_scatter x1, waiting for transfers between devices, on_device(): lax.psum_scatter(input_term.astype(BF16), 'head', scatter_dimension=1, ti...  19 us
    all_gather x1, blocking collectives, on_device(): lax.all_gather(term.reshape(part_rows, half_width), 'x', axis=0, tiled=True)  13.4 us
    all_to_all x1, waiting for transfers between devices, on_device(): parts = lax.all_to_all(pair_sum.astype(BF16), 'x', 0, 0, tiled=True)  12.8 us
    all_to_all x1, waiting for transfers between devices, sum_parts(): got = lax.all_to_all(value, axis, 0, 0, tiled=True)  10.8 us
    all_to_all x1, waiting for transfers between devices, on_device(): mine = lax.all_to_all(copies, 'x', 0, 0, tiled=True)  9.43 us
    all_to_all x1, starting transfers between devices, on_device(): mine = lax.all_to_all(copies, 'x', 0, 0, tiled=True)  9.39 us
    all_to_all x1, waiting for transfers between devices, on_device(): term = lax.all_to_all(term, 'interval', 0, 0, tiled=True)  7.32 us
  transfers between devices with their start and end apart: 8, of which 7 were waited for; matrix products, arithmetic and copies ran while one was open for 10% of the time, Pallas kernels for 0%

commit v1 on v0

--- a/solution.py
+++ b/solution.py
@@ -118,7 +118,9 @@
     term = jnp.broadcast_to(term[None], (intervals,) + term.shape).reshape(-1, cut[3])
     term = lax.all_to_all(term, "interval", 0, 0, tiled=True)
     term = term.reshape(cut[0], cut[2], cut[1], cut[3]).transpose(0, 2, 1, 3)
-    term = lax.all_gather(term.reshape(part_rows, half_width), "x", axis=0, tiled=True)
+    part = term.reshape(part_rows, half_width)
+    repeated = jnp.stack([part] * lax.axis_size("x"))
+    term = jnp.concatenate(lax.all_to_all(repeated, "x", 0, 0), axis=0)
     other = swap_cores(term)
     left = jnp.where(core == 0, term, other)
     right = jnp.where(core == 0, other, term)

time: 190 us -> 202 us (1.063)
  waiting for transfers between devices: 64 us -> 72.6 us
  blocking collectives: 35 us -> 40.1 us
    all_to_all x2 -> x3, blocking collectives: 21.6 us -> 40.1 us  [sum_parts(): got = lax.all_to_all(value, axis, 0, 0, tiled=True)]
    all_gather x1 -> x0, blocking collectives: 13.4 us -> none  [on_device(): lax.all_gather(term.reshape(part_rows, half_width), 'x', axis=0, tiled=True)]
    reduce_scatter x1, waiting for transfers between devices: 19 us -> 31.1 us  [on_device(): lax.psum_scatter(input_term.astype(BF16), 'head', scatter_dimension=1, ti...]
    all_to_all x1, waiting for transfers between devices: 10.8 us -> 4 us  [on_device(): term = jnp.concatenate(lax.all_to_all(repeated, 'x', 0, 0), axis=0)]
    all_to_all x1, waiting for transfers between devices: 7.32 us -> 10.7 us  [on_device(): term = lax.all_to_all(term, 'interval', 0, 0, tiled=True)]
  transfers between devices with their start and end apart: 8 -> 8, of which waited for: 7 -> 7; matrix products, arithmetic and copies ran while one was open for 10% -> 9% of each run, Pallas kernels for 0% -> 0%
where the time goes in v1:
time: 202 us; the launch traced here: 201 us
  waiting for transfers between devices  72.6 us (36%)
  blocking collectives  40.1 us (20%)
  starting transfers between devices  29.6 us (15%)
  local copies, waits for them, and re-layouts  17.5 us (9%)
  between operations  14.5 us (7%)
  matrix products  13.8 us (7%)
  other arithmetic  13.3 us (7%)
    all_to_all x3, blocking collectives, sum_parts(): got = lax.all_to_all(value, axis, 0, 0, tiled=True)  40.1 us
    reduce_scatter x1, waiting for transfers between devices, on_device(): lax.psum_scatter(input_term.astype(BF16), 'head', scatter_dimension=1, ti...  31.1 us
    all_to_all x1, waiting for transfers between devices, on_device(): parts = lax.all_to_all(pair_sum.astype(BF16), 'x', 0, 0, tiled=True)  12.8 us
    all_to_all x1, waiting for transfers between devices, on_device(): term = lax.all_to_all(term, 'interval', 0, 0, tiled=True)  10.7 us
    all_to_all x1, waiting for transfers between devices, on_device(): mine = lax.all_to_all(copies, 'x', 0, 0, tiled=True)  9.43 us
    all_to_all x1, starting transfers between devices, on_device(): mine = lax.all_to_all(copies, 'x', 0, 0, tiled=True)  9.39 us
    ppermute x3, starting transfers between devices, swap_cores(): return lax.ppermute(value, 'core', [(0, 1), (1, 0)])  6.22 us
    all_to_all x1, starting transfers between devices, on_device(): parts = lax.all_to_all(pair_sum.astype(BF16), 'x', 0, 0, tiled=True)  5.68 us
  transfers between devices with their start and end apart: 8, of which 7 were waited for; matrix products, arithmetic and copies ran while one was open for 9% of the time, Pallas kernels for 0%

profile of v1, /device:TPU:2, one launch (start us, length us, event | category | flops | bytes accessed | tf_op | source)
XLA Modules:
  0.0 201.4 jit_solution(5144197465520426676)
XLA Ops:
  7.2 1.1 copy-done
  8.3 1.4 convolution_convert_fusion.5
  9.7 1.5 convolution_convert_fusion.2
  12.9 9.4 %all-to-all-start = ((bf16[4,256,512]{2,1,0:T(8,128)(2,1)}), bf16[4,256,512]{2,1,0:T(8,128)(2,1)S(1)}, u32[]{:S(2)}, u32[]{:S(2)}) async-start(bf16[4,256,512]{2,1,0:T(8,128)(2,1)} %broadcast_in_dim.17), calls=%async_computation | async-start | bytes 2097152 | tf_op jit(solution)/shard_map/all_to_all | solution.py:47
  22.3 9.4 %all-to-all-done = bf16[4,256,512]{2,1,0:T(8,128)(2,1)S(1)} async-done(((bf16[4,256,512]{2,1,0:T(8,128)(2,1)}), bf16[4,256,512]{2,1,0:T(8,128)(2,1)S(1)}, u32[]{:S(2)}, u32[]{:S(2)}) %all-to-all-start) | async-done | bytes 1048608 | tf_op jit(solution)/shard_map/all_to_all | solution.py:47
  31.7 1.9 collective-permute-start
  41.3 1.3 pad_clamp_fusion
  42.5 1.2 fusion.33
  45.6 1.5 convolution_convert_fusion.1
  49.7 1.3 fusion.1
  51.9 2.0 %scatter_custom_fusion = f32[2048,128]{1,0:T(8,128)} fusion(s32[64]{0:T(128)} %fusion.33, f32[]{:T(128)} %constant.30.clone.1, bf16[64,128]{1,0:T(8,128)(2,1)S(1)} %gather_fusion, f32[64]{0:T(128)S(1)} %fusion.35), kind=kCustom, calls=%fused_computation.56 | custom fusion | flops 24576 | bytes 1065728 | tf_op jit(solution)/shard_map/scatter-add | solution.py:87
  53.9 1.4 copy.45
  55.3 1.5 pad_maximum_fusion
  57.0 2.4 %collective-permute-start.1 = (bf16[1024,512]{0,1:T(8,128)(2,1)S(1)}, bf16[1024,512]{0,1:T(8,128)(2,1)S(1)}, u32[]{:S(2)}, u32[]{:S(2)}) collective-permute-start(bf16[1024,512]{0,1:T(8,128)(2,1)S(1)} %slice.56), channel_id=1, source_target_pairs={{0,8},{8,0},{1,9},{9,1},{2,10},{10,2},{3,11},{11,3},{4,12},{12,4},... | collective-permute-start | bytes 3145736 | tf_op jit(solution)/shard_map/ppermute | solution.py:15
  59.4 2.3 %collective-permute-done.1 = bf16[1024,512]{0,1:T(8,128)(2,1)S(1)} collective-permute-done((bf16[1024,512]{0,1:T(8,128)(2,1)S(1)}, bf16[1024,512]{0,1:T(8,128)(2,1)S(1)}, u32[]{:S(2)}, u32[]{:S(2)}) %collective-permute-start.1) | collective-permute-done | bytes 1048608 | tf_op jit(solution)/shard_map/ppermute | solution.py:15
  63.1 5.7 %all-to-all-start.1 = ((bf16[4,256,512]{1,2,0:T(8,128)(2,1)}), bf16[4,256,512]{1,2,0:T(8,128)(2,1)}, u32[]{:S(2)}, u32[]{:S(2)}) async-start(bf16[4,256,512]{1,2,0:T(8,128)(2,1)} %bitcast.82), calls=%async_computation.1 | async-start | bytes 2097152 | tf_op jit(solution)/shard_map/all_to_all | solution.py:91
  68.8 1.8 fusion.10
  70.6 12.8 %all-to-all-done.1 = bf16[4,256,512]{1,2,0:T(8,128)(2,1)} async-done(((bf16[4,256,512]{1,2,0:T(8,128)(2,1)}), bf16[4,256,512]{1,2,0:T(8,128)(2,1)}, u32[]{:S(2)}, u32[]{:S(2)}) %all-to-all-start.1) | async-done | bytes 1048608 | tf_op jit(solution)/shard_map/all_to_all | solution.py:91
  83.3 1.4 convert_reduce_fusion
  86.4 5.2 %all_to_all.53 = bf16[2,576,768]{2,1,0:T(8,128)(2,1)S(1)} all-to-all(bf16[2,576,768]{2,1,0:T(8,128)(2,1)S(1)} %bitcast.79), channel_id=1, replica_groups=mesh['interval'=8,'x'=4,'core'=2,'head'=8] {'core'}, dimensions={0} | all-to-all | bytes 3538944 | tf_op jit(solution)/shard_map/all_to_all | solution.py:108
  92.4 16.3 %all_to_all.54 = bf16[4,144,768]{2,1,0:T(8,128)(2,1)S(1)} all-to-all(bf16[4,144,768]{2,1,0:T(8,128)(2,1)S(1)} %bitcast.83), channel_id=1, replica_groups=mesh['interval'=8,'x'=4,'core'=2,'head'=8] {'x'}, dimensions={0} | all-to-all | bytes 1769472 | tf_op jit(solution)/shard_map/all_to_all | solution.py:108
  109.2 18.6 %all_to_all.55 = bf16[8,72,192]{2,1,0:T(8,128)(2,1)S(1)} all-to-all(bf16[8,72,192]{2,1,0:T(8,128)(2,1)S(1)} %bitcast.86), channel_id=1, replica_groups=mesh['interval'=8,'x'=4,'core'=2,'head'=8] {'interval'}, dimensions={0} | all-to-all | bytes 442368 | tf_op jit(solution)/shard_map/all_to_all | solution.py:108
  128.6 3.4 %all-to-all-start.5 = ((bf16[8,72,192]{2,1,0:T(8,128)(2,1)}), bf16[8,72,192]{2,1,0:T(8,128)(2,1)S(1)}, u32[]{:S(2)}, u32[]{:S(2)}) async-start(bf16[8,72,192]{2,1,0:T(8,128)(2,1)} %broadcast_in_dim.23), calls=%async_computation.6 | async-start | bytes 589824 | tf_op jit(solution)/shard_map/all_to_all | solution.py:119
  132.1 10.7 %all-to-all-done.5 = bf16[8,72,192]{2,1,0:T(8,128)(2,1)S(1)} async-done(((bf16[8,72,192]{2,1,0:T(8,128)(2,1)}), bf16[8,72,192]{2,1,0:T(8,128)(2,1)S(1)}, u32[]{:S(2)}, u32[]{:S(2)}) %all-to-all-start.5) | async-done | bytes 221216 | tf_op jit(solution)/shard_map/all_to_all | solution.py:119
  144.2 4.9 %all-to-all-start.6 = ((bf16[4,144,768]{2,1,0:T(8,128)(2,1)}), bf16[4,144,768]{2,1,0:T(8,128)(2,1)S(1)}, u32[]{:S(2)}, u32[]{:S(2)}) async-start(bf16[4,144,768]{2,1,0:T(8,128)(2,1)} %stack.3), calls=%async_computation.7 | async-start | bytes 1769472 | tf_op jit(solution)/shard_map/all_to_all | solution.py:123
  150.4 2.1 %fusion.4 = f32[256,1536]{0,1:T(8,128)S(1)} fusion(bf16[192,1536]{1,0:T(8,128)(2,1)S(1)} %copy-done.6, bf16[192,1536]{1,0:T(8,128)(2,1)S(1)} %copy-done.8, bf16[192,1536]{1,0:T(8,128)(2,1)} %param.12, bf16[256,384]{0,1:T(8,128)(2,1)S(1)} %copy-done.5, bf16[256,192]{0,1:T(8,128)(2,1)S(1)} %fusion.10), kind=kOutput, calls=%fused_computation.29 | convolution fusion | flops 458883072 | bytes 3637248 | tf_op jit(solution)/shard_map/dot_general | solution.py:98
  152.4 1.3 fusion
  153.8 4.0 %all-to-all-done.6 = bf16[4,144,768]{2,1,0:T(8,128)(2,1)S(1)} async-done(((bf16[4,144,768]{2,1,0:T(8,128)(2,1)}), bf16[4,144,768]{2,1,0:T(8,128)(2,1)S(1)}, u32[]{:S(2)}, u32[]{:S(2)}) %all-to-all-start.6) | async-done | bytes 884768 | tf_op jit(solution)/shard_map/all_to_all | solution.py:123
  157.8 1.9 collective-permute-start.2
  159.7 2.4 %collective-permute-done.2 = bf16[576,768]{1,0:T(8,128)(2,1)S(1)} collective-permute-done((bf16[576,768]{1,0:T(8,128)(2,1)S(1)}, bf16[576,768]{1,0:T(8,128)(2,1)S(1)}, u32[]{:S(2)}, u32[]{:S(2)}) %collective-permute-start.2) | collective-permute-done | bytes 884768 | tf_op jit(solution)/shard_map/ppermute | solution.py:15
  162.2 1.2 pad_maximum_fusion.1
  163.5 31.1 %reduce-scatter.2.cloned.1.call-done = bf16[256,192]{0,1:T(8,128)(2,1)} async-done(((bf16[256,1536]{0,1:T(8,128)(2,1)}), bf16[256,192]{0,1:T(8,128)(2,1)}) %reduce-scatter.2.cloned.1.call-update) | async-done | bytes 98320 | tf_op jit(solution)/shard_map/reduce_scatter | solution.py:102
  (100 shorter events, 22.6 us)
Async XLA Ops:
  7.2 1.1 copy-start
  7.2 4.0 %copy-start.7 = (bf16[192,1536]{1,0:T(8,128)(2,1)S(1)}, bf16[192,1536]{1,0:T(8,128)(2,1)}, u32[]{:S(2)}) copy-start(bf16[192,1536]{1,0:T(8,128)(2,1)} %param.13) | copy-start | bytes 1769476
  9.7 1.9 copy-start.10
  11.7 22.0 %copy-start.12 = (s32[1,1,8,8]{3,2,1,0:T(8,128)S(1)}, s32[1,1,8,8]{3,2,1,0:T(8,128)}, u32[]{:S(2)}) copy-start(s32[1,1,8,8]{3,2,1,0:T(8,128)} %param.17) | copy-start | bytes 772
  11.7 24.2 %copy-start.13 = (s32[1,1,8,8]{3,2,1,0:T(8,128)S(1)}, s32[1,1,8,8]{3,2,1,0:T(8,128)}, u32[]{:S(2)}) copy-start(s32[1,1,8,8]{3,2,1,0:T(8,128)} %param.16) | copy-start | bytes 772
  11.7 26.3 %copy-start.17 = (f32[1,1,8,8]{3,2,1,0:T(8,128)S(1)}, f32[1,1,8,8]{3,2,1,0:T(8,128)}, u32[]{:S(2)}) copy-start(f32[1,1,8,8]{3,2,1,0:T(8,128)} %param.19) | copy-start | bytes 772
  11.7 32.0 %copy-start.9 = (bf16[192,1536]{1,0:T(8,128)(2,1)S(1)}, bf16[192,1536]{1,0:T(8,128)(2,1)}, u32[]{:S(2)}) copy-start(bf16[192,1536]{1,0:T(8,128)(2,1)} %param.12) | copy-start | bytes 1769476
  12.9 18.8 %all-to-all-start = ((bf16[4,256,512]{2,1,0:T(8,128)(2,1)}), bf16[4,256,512]{2,1,0:T(8,128)(2,1)S(1)}, u32[]{:S(2)}, u32[]{:S(2)}) async-start(bf16[4,256,512]{2,1,0:T(8,128)(2,1)} %broadcast_in_dim.17), calls=%async_computation | async-start | bytes 2097152 | tf_op jit(solution)/shard_map/all_to_all | solution.py:47
  22.3 11.4 %copy-start.21 = (s32[8]{0:T(128)}, s32[8]{0:T(128)S(1)}, u32[]{:S(2)}) copy-start(s32[8]{0:T(128)S(1)} %fusion.31) | copy-start | bytes 100
  31.7 12.4 %collective-permute-start = (bf16[1024,512]{1,0:T(8,128)(2,1)S(1)}, bf16[1024,512]{1,0:T(8,128)(2,1)S(1)}, u32[]{:S(2)}, u32[]{:S(2)}) collective-permute-start(bf16[1024,512]{1,0:T(8,128)(2,1)S(1)} %bitcast.74), channel_id=1, source_target_pairs={{0,8},{8,0},{1,9},{9,1},{2,10},{10,2},{3,11},{11,3},{4,12},{12,4},... | collective-permute-start | bytes 3145736 | tf_op jit(solution)/shard_map/ppermute | solution.py:15
  44.7 0.9 copy-start.22
  48.7 1.0 copy-start.1
  49.7 1.4 copy-start.11
  49.7 2.1 %copy-start.18 = (s32[64]{0:T(128)S(1)}, s32[64]{0:T(128)}, u32[]{:S(2)}) copy-start(s32[64]{0:T(128)} %lt.72) | copy-start | bytes 772
  49.7 2.1 %copy-start.19 = (s32[64]{0:T(128)S(1)}, s32[64]{0:T(128)}, u32[]{:S(2)}) copy-start(s32[64]{0:T(128)} %lt.75) | copy-start | bytes 772
  49.7 2.1 %copy-start.20 = (f32[64]{0:T(128)S(1)}, f32[64]{0:T(128)}, u32[]{:S(2)}) copy-start(f32[64]{0:T(128)} %squeeze.20) | copy-start | bytes 772
  51.9 5.0 %copy-start.15 = (f32[64]{0:T(128)}, f32[64]{0:T(128)S(1)}, u32[]{:S(2)}) copy-start(f32[64]{0:T(128)S(1)} %fusion.35) | copy-start | bytes 772
  57.0 4.7 %collective-permute-start.1 = (bf16[1024,512]{0,1:T(8,128)(2,1)S(1)}, bf16[1024,512]{0,1:T(8,128)(2,1)S(1)}, u32[]{:S(2)}, u32[]{:S(2)}) collective-permute-start(bf16[1024,512]{0,1:T(8,128)(2,1)S(1)} %slice.56), channel_id=1, source_target_pairs={{0,8},{8,0},{1,9},{9,1},{2,10},{10,2},{3,11},{11,3},{4,12},{12,4},... | collective-permute-start | bytes 3145736 | tf_op jit(solution)/shard_map/ppermute | solution.py:15
  63.1 20.2 %all-to-all-start.1 = ((bf16[4,256,512]{1,2,0:T(8,128)(2,1)}), bf16[4,256,512]{1,2,0:T(8,128)(2,1)}, u32[]{:S(2)}, u32[]{:S(2)}) async-start(bf16[4,256,512]{1,2,0:T(8,128)(2,1)} %bitcast.82), calls=%async_computation.1 | async-start | bytes 2097152 | tf_op jit(solution)/shard_map/all_to_all | solution.py:91
  84.8 0.8 copy-start.3
  85.6 0.7 copy-start.4
  108.8 23.3 %copy-start.14 = (s32[1,1,8,8]{3,2,1,0:T(8,128)S(1)}, s32[1,1,8,8]{3,2,1,0:T(8,128)}, u32[]{:S(2)}) copy-start(s32[1,1,8,8]{3,2,1,0:T(8,128)} %param.16) | copy-start | bytes 772
  128.6 14.2 %all-to-all-start.5 = ((bf16[8,72,192]{2,1,0:T(8,128)(2,1)}), bf16[8,72,192]{2,1,0:T(8,128)(2,1)S(1)}, u32[]{:S(2)}, u32[]{:S(2)}) async-start(bf16[8,72,192]{2,1,0:T(8,128)(2,1)} %broadcast_in_dim.23), calls=%async_computation.6 | async-start | bytes 589824 | tf_op jit(solution)/shard_map/all_to_all | solution.py:119
  142.8 6.4 %slice-start = ((f32[256,512]{0,1:T(8,128)}), f32[256,128]{0,1:T(8,128)S(1)}, s32[]{:S(2)}) async-start(f32[256,512]{0,1:T(8,128)} %copy-done.3), calls=%async_computation.9 | async-start | bytes 262144 | tf_op jit(solution)/shard_map/slice | solution.py:95
  142.9 6.3 %copy-start.16 = (f32[64]{0:T(128)S(1)}, f32[64]{0:T(128)}, u32[]{:S(2)}) copy-start(f32[64]{0:T(128)} %copy-done.15) | copy-start | bytes 772
  142.9 7.4 %copy-start.5 = (bf16[256,384]{0,1:T(8,128)(2,1)S(1)}, bf16[256,384]{0,1:T(8,128)(2,1)}, u32[]{:S(2)}) copy-start(bf16[256,384]{0,1:T(8,128)(2,1)} %copy-done.4) | copy-start | bytes 589828
  142.9 7.4 %copy-start.6 = (bf16[192,1536]{1,0:T(8,128)(2,1)S(1)}, bf16[192,1536]{1,0:T(8,128)(2,1)}, u32[]{:S(2)}) copy-start(bf16[192,1536]{1,0:T(8,128)(2,1)} %param.14) | copy-start | bytes 1769476
  142.9 7.4 %copy-start.8 = (bf16[192,1536]{1,0:T(8,128)(2,1)S(1)}, bf16[192,1536]{1,0:T(8,128)(2,1)}, u32[]{:S(2)}) copy-start(bf16[192,1536]{1,0:T(8,128)(2,1)} %param.13) | copy-start | bytes 1769476
  144.2 13.6 %all-to-all-start.6 = ((bf16[4,144,768]{2,1,0:T(8,128)(2,1)}), bf16[4,144,768]{2,1,0:T(8,128)(2,1)S(1)}, u32[]{:S(2)}, u32[]{:S(2)}) async-start(bf16[4,144,768]{2,1,0:T(8,128)(2,1)} %stack.3), calls=%async_computation.7 | async-start | bytes 1769472 | tf_op jit(solution)/shard_map/all_to_all | solution.py:123
  149.1 45.4 %reduce-scatter.2.cloned.1.call-start = ((), (), s32[]{:S(2)}) async-start(), calls=%async_computation.8 | async-start | bytes 884736 | tf_op jit(solution)/shard_map/reduce_scatter | solution.py:102
  150.3 2.1 %copy-start.2 = (bf16[1536,128]{1,0:T(8,128)(2,1)S(1)}, bf16[1536,128]{1,0:T(8,128)(2,1)}, u32[]{:S(2)}) copy-start(bf16[1536,128]{1,0:T(8,128)(2,1)} %param.15) | copy-start | bytes 1179652
  157.8 4.3 %collective-permute-start.2 = (bf16[576,768]{1,0:T(8,128)(2,1)S(1)}, bf16[576,768]{1,0:T(8,128)(2,1)S(1)}, u32[]{:S(2)}, u32[]{:S(2)}) collective-permute-start(bf16[576,768]{1,0:T(8,128)(2,1)S(1)} %bitcast.84), channel_id=1, source_target_pairs={{0,8},{8,0},{1,9},{9,1},{2,10},{10,2},{3,11},{11,3},{4,12},{12,4},... | collective-permute-start | bytes 2654216 | tf_op jit(solution)/shard_map/ppermute | solution.py:15
Sparse Core Ops, SparseCore 0:
  153.9 40.6 reduce-scatter.1
